TPU v7x, 32 devices: a whole 2x2x4 slice. The times are simulated.
32 devices in a mesh: dp: 2 (over x), row: 4 (over z), col: 4 (over y, core).
Axes of the slice: x: 2, y: 2, z: 4, core: 2. Of those that a mesh axis runs over, the one named last changes fastest.
Arguments:
- hidden_in: bfloat16 [4096, 1024], P(('dp', 'row'), 'col'), may hold values from -18 to 18
- doc_ids: int32 [8, 512], P(('dp', 'row')), may hold values from 0 to 3, as said below
- w_qkv: bfloat16 [1024, 3, 1024], P('row', None, 'col'), may hold values from -0.1875 to 0.1875
- query_bias: float32 [1024], P('col'), may hold values from -3 to 3
- value_bias: float32 [1024], P('col'), may hold values from -3 to 3
- w_out: bfloat16 [1024, 1024], P('col', 'row'), may hold values from -0.75 to 0.75
- out_bias: float32 [1024], P('col'), may hold values from -3 to 3
- norm_gain: float32 [1024], P('col'), may hold values from 0.5 to 1.5
- norm_shift: float32 [1024], P('col'), may hold values from -3 to 3
- w_up: bfloat16 [1024, 4096], P('row', 'col'), may hold values from -0.1875 to 0.1875
- up_bias: float32 [4096], P('col'), may hold values from -3 to 3
- w_down: bfloat16 [4096, 1024], P('col', 'row'), may hold values from -0.09375 to 0.09375
- down_bias: float32 [1024], P('col'), may hold values from -3 to 3
- final_gain: float32 [1024], P('col'), may hold values from 0.5 to 1.5
- final_shift: float32 [1024], P('col'), may hold values from -3 to 3
- out_grad: bfloat16 [4096, 1024], P(('dp', 'row'), 'col'), may hold values from -6 to 6
Outputs:
- layer_out: bfloat16 [4096, 1024], P(('dp', 'row'), 'col')
- hidden_grad: float32 [4096, 1024], P(('dp', 'row'), 'col')
- wqkv_grad: float32 [1024, 3, 1024], P('row', None, 'col')
- qbias_grad: float32 [1024], P('col')
- vbias_grad: float32 [1024], P('col')
- wout_grad: float32 [1024, 1024], P('col', 'row')
- obias_grad: float32 [1024], P('col')
- ngain_grad: float32 [1024], P('col')
- nshift_grad: float32 [1024], P('col')
- wup_grad: float32 [1024, 4096], P('row', 'col')
- ubias_grad: float32 [4096], P('col')
- wdown_grad: float32 [4096, 1024], P('col', 'row')
- dbias_grad: float32 [1024], P('col')
- fgain_grad: float32 [1024], P('col')
- fshift_grad: float32 [1024], P('col')
Inputs may be any that keep to these rules, and one draw needn't show every extreme that they name: `doc_ids`: along each sequence the ids never fall, start at 0 and end at 3: every sequence packs four documents, each of 51 tokens or more.
All inputs are finite; a program needn't handle non-finite values.
Results may differ from a plain program's by a relative error of at most 0.015.
Values may be sent and summed in bfloat16 or wider, within the bound.
A program may use at most 128 MiB of HBM per device.

v0:
```python
import jax
import jax.numpy as jnp
from jax import lax
from jax.sharding import PartitionSpec as P

D = 1024
HD = 64
EPS = 1e-12
INV_ROOT_TWO = 0.7071067811865476
INV_ROOT_PI = 0.3989422804014327


def gelu_parts(pre_act):
    cdf_val = 0.5 * (1.0 + lax.erf(pre_act * INV_ROOT_TWO))
    density = jnp.exp(-0.5 * pre_act * pre_act) * INV_ROOT_PI
    return (pre_act * cdf_val, cdf_val + pre_act * density)


def normalize(total, gain, shift):
    mean_val = lax.psum(jnp.sum(total, axis=1), "col") / D
    centered = total - mean_val[:, None]
    variance = lax.psum(jnp.sum(centered * centered, axis=1), "col") / D
    inverse = lax.rsqrt(variance + EPS)[:, None]
    normed = centered * inverse
    return (normed * gain + shift, normed, inverse)


def norm_back(upstream, normed, inverse, gain):
    scaled = upstream * gain
    first_sum, second = lax.psum((jnp.sum(scaled, axis=1), jnp.sum(scaled * normed, axis=1)), "col")
    return inverse * (scaled - first_sum[:, None] / D - normed * (second[:, None] / D))


def spread(block):
    return lax.all_gather(block, "col", axis=1, tiled=True)


def spread_grad(block):
    return lax.all_gather(block, "col", axis=1, tiled=True)


def collect(partial_sum):
    return lax.psum_scatter(partial_sum, "col", scatter_dimension=1, tiled=True)


def collect_back(partial_sum):
    return lax.psum_scatter(partial_sum, "col", scatter_dimension=1, tiled=True)


def seq_scores(query, keys, doc_row):
    same_doc = doc_row[:, None] == doc_row[None, :]
    scores = jnp.einsum("qhd,khd->hqk", query, keys, preferred_element_type=jnp.float32) * HD ** (
        -0.5
    )
    return jnp.where(same_doc[None], scores, -jnp.inf)


def attend_seq(inputs_seq):
    query, keys, values, doc_row = inputs_seq
    scores = seq_scores(query, keys, doc_row)
    top_score = jnp.max(scores, axis=-1, keepdims=True)
    log_total = top_score + jnp.log(jnp.sum(jnp.exp(scores - top_score), axis=-1, keepdims=True))
    prob_bf = jnp.exp(scores - log_total).astype(jnp.bfloat16)
    context = jnp.einsum(
        "hqk,khd->qhd", prob_bf, values, preferred_element_type=jnp.float32
    ).astype(jnp.bfloat16)
    return (context, log_total)


def attend_back(inputs_seq):
    query, keys, values, doc_row, ctx_back, log_total = inputs_seq
    prob_f = jnp.exp(seq_scores(query, keys, doc_row) - log_total)
    v_back = jnp.einsum(
        "hqk,qhd->khd", prob_f.astype(jnp.bfloat16), ctx_back, preferred_element_type=jnp.float32
    )
    d_prob = jnp.einsum("qhd,khd->hqk", ctx_back, values, preferred_element_type=jnp.float32)
    row_delta = jnp.sum(prob_f * d_prob, axis=-1, keepdims=True)
    score_back = (prob_f * (d_prob - row_delta) * HD ** (-0.5)).astype(jnp.bfloat16)
    q_back = jnp.einsum("hqk,khd->qhd", score_back, keys, preferred_element_type=jnp.float32)
    k_back = jnp.einsum("hqk,qhd->khd", score_back, query, preferred_element_type=jnp.float32)
    return (q_back, k_back, v_back)


def per_device(
    hidden_in,
    doc_ids,
    w_qkv,
    query_bias,
    value_bias,
    w_out,
    out_bias,
    norm_gain,
    norm_shift,
    w_up,
    up_bias,
    w_down,
    down_bias,
    final_gain,
    final_shift,
    out_grad,
):
    f32 = jnp.float32
    bf16 = jnp.bfloat16
    qkv_full, out_full, up_full, down_full = (
        lax.all_gather(w_qkv, "row", axis=0, tiled=True),
        lax.all_gather(w_out, "row", axis=1, tiled=True),
        lax.all_gather(w_up, "row", axis=0, tiled=True),
        lax.all_gather(w_down, "row", axis=1, tiled=True),
    )
    tokens_dev = hidden_in.shape[0]
    col_width = hidden_in.shape[1]
    head_count = col_width // HD
    seq_count = doc_ids.shape[0]
    seq_len = doc_ids.shape[1]
    head_shape = (seq_count, seq_len, head_count, HD)
    x_full = spread(hidden_in)
    projected = jnp.einsum("td,dkc->tkc", x_full, qkv_full, preferred_element_type=f32)
    query = (projected[:, 0] + query_bias).astype(bf16).reshape(head_shape)
    keys = projected[:, 1].astype(bf16).reshape(head_shape)
    values = (projected[:, 2] + value_bias).astype(bf16).reshape(head_shape)
    context, log_total = lax.map(attend_seq, (query, keys, values, doc_ids))
    ctx_rows = context.reshape(tokens_dev, col_width)
    total_one = (
        hidden_in.astype(f32)
        + collect(jnp.dot(ctx_rows, out_full, preferred_element_type=f32))
        + out_bias
    )
    attn_act, normed_one, inverse_one = normalize(total_one, norm_gain, norm_shift)
    attn_bf = attn_act.astype(bf16)
    attn_full = spread(attn_bf)
    up_pre = jnp.dot(attn_full, up_full, preferred_element_type=f32) + up_bias
    act_f, slope = gelu_parts(up_pre)
    act = act_f.astype(bf16)
    total_two = attn_act + collect(jnp.dot(act, down_full, preferred_element_type=f32)) + down_bias
    final, normed_two, inverse_two = normalize(total_two, final_gain, final_shift)
    layer_out = final.astype(bf16)
    grad_top = out_grad.astype(f32)
    fgain_part = jnp.sum(grad_top * normed_two, axis=0)
    fshift_part = jnp.sum(grad_top, axis=0)
    back_two = norm_back(grad_top, normed_two, inverse_two, final_gain)
    back_two_full = spread_grad(back_two.astype(bf16))
    wdown_part = jnp.dot(act.T, back_two_full, preferred_element_type=f32)
    dbias_part = jnp.sum(back_two, axis=0)
    up_back = jnp.dot(back_two_full, down_full.T, preferred_element_type=f32) * slope
    up_back_bf = up_back.astype(bf16)
    wup_part = jnp.dot(attn_full.T, up_back_bf, preferred_element_type=f32)
    ubias_part = jnp.sum(up_back, axis=0)
    attn_back = back_two + collect_back(jnp.dot(up_back_bf, up_full.T, preferred_element_type=f32))
    ngain_part = jnp.sum(attn_back * normed_one, axis=0)
    nshift_part = jnp.sum(attn_back, axis=0)
    back_one = norm_back(attn_back, normed_one, inverse_one, norm_gain)
    back_one_full = spread_grad(back_one.astype(bf16))
    wout_part = jnp.dot(ctx_rows.T, back_one_full, preferred_element_type=f32)
    obias_part = jnp.sum(back_one, axis=0)
    ctx_back = (
        jnp.dot(back_one_full, out_full.T, preferred_element_type=f32)
        .astype(bf16)
        .reshape(head_shape)
    )
    q_back, k_back, v_back = lax.map(
        attend_back, (query, keys, values, doc_ids, ctx_back, log_total)
    )
    q_back = q_back.reshape(tokens_dev, col_width)
    k_back = k_back.reshape(tokens_dev, col_width)
    v_back = v_back.reshape(tokens_dev, col_width)
    qbias_part = jnp.sum(q_back, axis=0)
    vbias_part = jnp.sum(v_back, axis=0)
    qkv_back = jnp.stack([q_back, k_back, v_back], axis=1).astype(bf16)
    wqkv_part = jnp.einsum("td,tkc->dkc", x_full, qkv_back, preferred_element_type=f32)
    hidden_grad = back_one + collect_back(
        jnp.einsum("tkc,dkc->td", qkv_back, qkv_full, preferred_element_type=f32)
    )
    pieces = (
        lax.psum_scatter(
            wqkv_part.astype(jnp.bfloat16), "row", scatter_dimension=0, tiled=True
        ).astype(jnp.float32),
        lax.psum_scatter(
            wout_part.astype(jnp.bfloat16), "row", scatter_dimension=1, tiled=True
        ).astype(jnp.float32),
        lax.psum_scatter(
            wup_part.astype(jnp.bfloat16), "row", scatter_dimension=0, tiled=True
        ).astype(jnp.float32),
        lax.psum_scatter(
            wdown_part.astype(jnp.bfloat16), "row", scatter_dimension=1, tiled=True
        ).astype(jnp.float32),
    )
    wqkv_grad, wout_grad, wup_grad, wdown_grad = (
        lax.psum(pieces[0].astype(jnp.bfloat16), "dp").astype(jnp.float32),
        lax.psum(pieces[1].astype(jnp.bfloat16), "dp").astype(jnp.float32),
        lax.psum(pieces[2].astype(jnp.bfloat16), "dp").astype(jnp.float32),
        lax.psum(pieces[3].astype(jnp.bfloat16), "dp").astype(jnp.float32),
    )
    small_sums = lax.psum(
        (
            qbias_part,
            vbias_part,
            obias_part,
            ngain_part,
            nshift_part,
            ubias_part,
            dbias_part,
            fgain_part,
            fshift_part,
        ),
        ("dp", "row"),
    )
    return (
        layer_out,
        hidden_grad,
        wqkv_grad,
        small_sums[0],
        small_sums[1],
        wout_grad,
        small_sums[2],
        small_sums[3],
        small_sums[4],
        wup_grad,
        small_sums[5],
        wdown_grad,
        small_sums[6],
        small_sums[7],
        small_sums[8],
    )


def solution(mesh):
    placed = (
        P(("dp", "row"), "col"),
        P(("dp", "row"), None),
        P("row", None, "col"),
        P("col"),
        P("col"),
        P("col", "row"),
        P("col"),
        P("col"),
        P("col"),
        P("row", "col"),
        P("col"),
        P("col", "row"),
        P("col"),
        P("col"),
        P("col"),
        P(("dp", "row"), "col"),
    )
    return jax.shard_map(
        per_device,
        mesh=mesh,
        in_specs=placed,
        out_specs=(
            P(("dp", "row"), "col"),
            P(("dp", "row"), "col"),
            P("row", None, "col"),
            P("col"),
            P("col"),
            P("col", "row"),
            P("col"),
            P("col"),
            P("col"),
            P("row", "col"),
            P("col"),
            P("col", "row"),
            P("col"),
            P("col"),
            P("col"),
        ),
        check_vma=False,
    )
```

profile of v0, /device:TPU:0, one launch (start us, length us, event | category | flops | bytes accessed | tf_op | source)
XLA Modules:
  0.0 611.3 jit_solution(2286843427765584200)
XLA Ops:
  7.2 0.7 all-gather.8.cloned.1.call-update
  8.0 1.9 copy.31
  9.9 0.8 add.163
  10.7 0.8 add.160
  11.5 17.6 %all_gather.26 = bf16[256,1024]{1,0:T(8,128)(2,1)S(1)} all-gather(bf16[256,256]{1,0:T(8,128)(2,1)} %param.21), channel_id=1, replica_groups=mesh['dp'=2,'row'=4,'col'=4] {'row'}, dimensions={1}, use_global_device_ids=true | all-gather | bytes 655360 | tf_op jit(solution)/shard_map/all_gather | solution.py:106
  29.0 1.0 broadcast_compare_fusion
  30.0 38.9 %all-gather.10.cloned.1.call-done = bf16[1024,3,256]{0,2,1:T(8,128)(2,1)} async-done(((bf16[256,3,256]{0,2,1:T(8,128)(2,1)}), bf16[1024,3,256]{0,2,1:T(8,128)(2,1)}) %all-gather.10.cloned.1.call-update) | async-done | bytes 1572880 | tf_op jit(solution)/shard_map/all_gather | solution.py:105
  69.0 2.7 fusion.26
  71.8 0.6 copy-done.2
  72.4 0.9 fusion.2
  73.4 0.9 exponential_reduce_fusion
  74.3 1.3 convolution_convert_fusion.5
  75.7 0.6 copy-done.6
  76.3 1.8 fusion.60
  78.8 28.9 %reduce-scatter.9.cloned.1.call-done = f32[512,256]{1,0:T(8,128)} async-done(((f32[512,1024]{1,0:T(8,128)}), f32[512,256]{1,0:T(8,128)}) %reduce-scatter.9.cloned.1.call-update) | async-done | bytes 524304 | tf_op jit(solution)/shard_map/reduce_scatter | solution.py:43
  107.7 1.2 fusion.53
  108.9 5.8 psum.147
  114.9 5.7 psum.148
  120.6 0.9 fusion.40
  121.5 0.5 all-gather.16.cloned.1.call-update
  122.1 32.7 %all-gather.14.cloned.1.call-done = bf16[1024,1024]{1,0:T(8,128)(2,1)} async-done(((bf16[256,1024]{1,0:T(8,128)(2,1)}), bf16[1024,1024]{1,0:T(8,128)(2,1)}) %all-gather.14.cloned.1.call-update) | async-done | bytes 2097168 | tf_op jit(solution)/shard_map/all_gather | solution.py:107
  154.8 17.6 %all-gather.12.cloned.1.call-done = bf16[512,1024]{1,0:T(8,128)(2,1)} async-done(((bf16[512,256]{1,0:T(8,128)(2,1)}), bf16[512,1024]{1,0:T(8,128)(2,1)}) %all-gather.12.cloned.1.call-update) | async-done | bytes 1048592 | tf_op jit(solution)/shard_map/all_gather | solution.py:35
  172.4 4.9 multiply_convert_fusion.1
  177.4 42.8 %all-gather.16.cloned.1.call-done = bf16[1024,1024]{1,0:T(8,128)(2,1)} async-done(((bf16[1024,256]{1,0:T(8,128)(2,1)}), bf16[1024,1024]{1,0:T(8,128)(2,1)}) %all-gather.16.cloned.1.call-update) | async-done | bytes 2097168 | tf_op jit(solution)/shard_map/all_gather | solution.py:108
  220.1 4.5 fusion.61
  224.7 29.4 %reduce-scatter.11.cloned.1.call-done = f32[512,256]{1,0:T(8,128)} async-done(((f32[512,1024]{1,0:T(8,128)}), f32[512,256]{1,0:T(8,128)}) %reduce-scatter.11.cloned.1.call-update) | async-done | bytes 524304 | tf_op jit(solution)/shard_map/reduce_scatter | solution.py:43
  254.2 1.3 fusion.52
  255.5 5.8 psum.149
  261.5 5.7 psum.150
  267.6 6.3 %all-reduce.2 = (f32[512]{0:T(512)S(1)}, f32[512]{0:T(512)S(1)}) all-reduce(f32[512]{0:T(512)S(1)} %get-tuple-element.84, f32[512]{0:T(512)S(1)} %get-tuple-element.87), channel_id=1, replica_groups=mesh['dp'=2,'row'=4,'col'=4] {'col'}, use_global_device_ids=true, to_apply=%region_15.16 | all-reduce | flops 1024 | bytes 8192 | tf_op jit(solution)/shard_map/psum | solution.py:30
  273.9 2.0 fusion.49
  275.9 0.7 convert_element_type.104
  276.9 17.4 %all-gather.18.cloned.1.call-done = bf16[512,1024]{1,0:T(8,128)(2,1)} async-done(((bf16[512,256]{1,0:T(8,128)(2,1)}), bf16[512,1024]{1,0:T(8,128)(2,1)}) %all-gather.18.cloned.1.call-update) | async-done | bytes 1048592 | tf_op jit(solution)/shard_map/all_gather | solution.py:39
  294.3 4.6 fusion.59
  298.9 1.0 copy-done.18
  299.9 2.6 fusion.38
  302.6 31.3 %reduce-scatter.13.cloned.1.call-done = f32[512,256]{1,0:T(8,128)} async-done(((f32[512,1024]{1,0:T(8,128)}), f32[512,256]{1,0:T(8,128)}) %reduce-scatter.13.cloned.1.call-update) | async-done | bytes 524304 | tf_op jit(solution)/shard_map/reduce_scatter | solution.py:47
  333.9 1.4 multiply_reduce_fusion.1
  335.3 5.8 all-reduce.1
  341.4 0.7 convert_element_type.106
  342.2 4.3 convolution_convert_fusion
  346.6 3.8 convolution_convert_fusion.1
  350.5 9.3 %all-gather.20.cloned.1.call-done = bf16[512,1024]{1,0:T(8,128)(2,1)} async-done(((bf16[512,256]{1,0:T(8,128)(2,1)}), bf16[512,1024]{1,0:T(8,128)(2,1)}) %all-gather.20.cloned.1.call-update) | async-done | bytes 1048592 | tf_op jit(solution)/shard_map/all_gather | solution.py:39
  359.8 1.8 convolution_convert_fusion.4
  361.6 0.7 copy-done.7
  362.3 4.1 fusion.55
  366.4 1.1 copy.38
  367.5 2.2 convolution_convert_fusion.3
  370.0 3.9 fusion.41
  373.9 8.8 %fusion.56 = (f32[4,64]{1,0:T(4,128)S(1)}, bf16[512,4,64]{0,2,1:T(8,128)(2,1)S(1)}) fusion(bf16[512,4,64]{0,2,1:T(8,128)(2,1)S(1)} %bitcast.55, f32[4,512,512]{1,2,0:T(8,128)} %fusion.41, f32[4,512]{1,0:T(4,128)S(1)} %log_add_fusion, f32[4,512,512]{1,2,0:T(8,128)} %copy-done, pred[512,512]{0,1:T(8,128)(4,1)S(1)} %broadcast_compare_fusion), kind=kOutput, calls=%fused_computation.90 | convolution fusion | flops 146016512 | bytes 9184256 | tf_op jit(solution)/shard_map/while/body/eval_jaxpr/hqk,khd->qhd/dot_general | solution.py:79
  382.9 7.5 %fusion.22 = bf16[4,64,512]{2,1,0:T(8,128)(2,1)S(1)} fusion(f32[4,512,512]{1,2,0:T(8,128)} %fusion.41, f32[512,4,64]{0,2,1:T(8,128)S(1)} %bitcast.51, f32[4,64]{1,0:T(4,128)S(1)} %add.163, f32[4,512,512]{1,2,0:T(8,128)} %copy-done, f32[4,512]{1,0:T(4,128)S(1)} %log_add_fusion, pred[512,512]{0,1:T(8,128)(4,1)S(1)} %broadcast_compare_fusion), kind=kOutput, calls=%fused_computation.28 | convolution fusion | flops 146147840 | bytes 9446400 | tf_op jit(solution)/shard_map/while/body/eval_jaxpr/hqk,qhd->khd/dot_general | solution.py:80
  390.6 2.2 fusion.18
  392.8 3.7 convolution_bitcast_fusion
  396.6 9.1 %reduce-scatter.23.cloned.1.call-done = bf16[1024,256]{1,0:T(8,128)(2,1)} async-done(((bf16[1024,1024]{1,0:T(8,128)(2,1)}), bf16[1024,256]{1,0:T(8,128)(2,1)}) %reduce-scatter.23.cloned.1.call-update) | async-done | bytes 524304 | tf_op jit(solution)/shard_map/reduce_scatter | solution.py:183
  405.7 45.0 %reduce-scatter.21.cloned.1.call-done = bf16[256,1024]{1,0:T(8,128)(2,1)} async-done(((bf16[1024,1024]{1,0:T(8,128)(2,1)}), bf16[256,1024]{1,0:T(8,128)(2,1)}) %reduce-scatter.21.cloned.1.call-update) | async-done | bytes 524304 | tf_op jit(solution)/shard_map/reduce_scatter | solution.py:180
  450.7 23.9 %reduce-scatter.19.cloned.1.call-done = bf16[256,256]{1,0:T(8,128)(2,1)} async-done(((bf16[256,1024]{1,0:T(8,128)(2,1)}), bf16[256,256]{1,0:T(8,128)(2,1)}) %reduce-scatter.19.cloned.1.call-update) | async-done | bytes 131088 | tf_op jit(solution)/shard_map/reduce_scatter | solution.py:177
  474.7 35.9 %reduce-scatter.17.cloned.1.call-done = bf16[256,3,256]{0,2,1:T(8,128)(2,1)} async-done(((bf16[1024,3,256]{0,2,1:T(8,128)(2,1)}), bf16[256,3,256]{0,2,1:T(8,128)(2,1)}) %reduce-scatter.17.cloned.1.call-update) | async-done | bytes 393232 | tf_op jit(solution)/shard_map/reduce_scatter | solution.py:174
  510.7 35.2 %all-reduce = (f32[256]{0:T(256)}, f32[256]{0:T(256)}, f32[256]{0:T(256)}, f32[256]{0:T(256)}, f32[256]{0:T(256)}, /*index=5*/f32[1024]{0:T(1024)}, f32[256]{0:T(256)}, f32[256]{0:T(256)}, f32[256]{0:T(256)}) all-reduce(f32[256]{0:T(256)S(1)} %reduce_sum.188, ...), channel_id=1, replica_groups=mesh['dp'=2,'row'=4,'col'=4] {'dp','row'}, use_global_device_ids=true, to_apply=%region_26.27 | all-reduce | flops 3072 | bytes 24576 | tf_op jit(solution)/shard_map/psum | solution.py:193
  546.0 1.9 add.185
  547.9 49.0 %all-reduce.6.cloned.1.call-done = (bf16[256,3,256]{0,2,1:T(8,128)(2,1)}, bf16[256,256]{1,0:T(8,128)(2,1)}, bf16[256,1024]{1,0:T(8,128)(2,1)}, bf16[1024,256]{1,0:T(8,128)(2,1)}) async-done(((bf16[256,3,256]{0,2,1:T(8,128)(2,1)}, bf16[256,256]{1,0:T(8,128)(2,1)}, bf16[256,1024]{1,0:T(8,128)(2,1)}, bf16[1024,256]{1,0:T(8,128)(2,1)}), (bf16[256,3,256]{0,2,1:T(8,128)(2,1)}, bf16[256,256]{1,0:T(8,128)(2,1)}, ...) | async-done | bytes 1572880 | tf_op jit(solution)/shard_map/psum | solution.py:188
  596.9 1.6 convert_element_type.113
  598.5 2.0 copy.41
  600.6 2.1 convert_element_type.115
  602.7 2.1 convert_element_type.117
  (84 shorter events, 3.7 us)
Async XLA Ops:
  7.2 22.9 %all-gather.8.cloned.1.call-start = ((), (), s32[]{:S(2)}) async-start(), calls=%async_computation.8 | async-start | bytes 1310720 | tf_op jit(solution)/shard_map/all_gather | solution.py:35
  7.9 61.1 %all-gather.10.cloned.1.call-start = ((), (), s32[]{:S(2)}) async-start(), calls=%async_computation.9 | async-start | bytes 1966080 | tf_op jit(solution)/shard_map/all_gather | solution.py:105
  9.9 97.8 %reduce-scatter.9.cloned.1.call-start = ((), (), s32[]{:S(2)}) async-start(), calls=%async_computation.10 | async-start | bytes 2621440 | tf_op jit(solution)/shard_map/reduce_scatter | solution.py:43
  71.8 0.7 copy-start.2
  73.4 2.2 copy-start
  75.6 0.7 copy-start.6
  75.6 32.1 %copy-start.4 = (bf16[512,256]{1,0:T(8,128)(2,1)S(1)}, bf16[512,256]{1,0:T(8,128)(2,1)}, u32[]{:S(2)}) copy-start(bf16[512,256]{1,0:T(8,128)(2,1)} %param.16) | copy-start | bytes 786436
  75.6 32.1 %copy-start.11 = (f32[256]{0:T(256)S(1)}, f32[256]{0:T(256)}, u32[]{:S(2)}) copy-start(f32[256]{0:T(256)} %param.22) | copy-start | bytes 3076
  75.6 44.9 %copy-start.8 = (f32[256]{0:T(256)S(1)}, f32[256]{0:T(256)}, u32[]{:S(2)}) copy-start(f32[256]{0:T(256)} %param.23) | copy-start | bytes 3076
  75.7 44.9 %copy-start.9 = (f32[256]{0:T(256)S(1)}, f32[256]{0:T(256)}, u32[]{:S(2)}) copy-start(f32[256]{0:T(256)} %param.24) | copy-start | bytes 3076
  76.3 96.1 %copy-start.17 = (f32[1024]{0:T(1024)S(1)}, f32[1024]{0:T(1024)}, u32[]{:S(2)}) copy-start(f32[1024]{0:T(1024)} %param.26) | copy-start | bytes 12292
  78.1 76.7 %all-gather.14.cloned.1.call-start = ((), (), s32[]{:S(2)}) async-start(), calls=%async_computation.12 | async-start | bytes 2621440 | tf_op jit(solution)/shard_map/all_gather | solution.py:107
  78.7 93.7 %all-gather.12.cloned.1.call-start = ((), (), s32[]{:S(2)}) async-start(), calls=%async_computation.11 | async-start | bytes 1310720 | tf_op jit(solution)/shard_map/all_gather | solution.py:35
  121.5 98.6 %all-gather.16.cloned.1.call-start = ((), (), s32[]{:S(2)}) async-start(), calls=%async_computation.13 | async-start | bytes 2621440 | tf_op jit(solution)/shard_map/all_gather | solution.py:108
  122.1 132.1 %reduce-scatter.11.cloned.1.call-start = ((), (), s32[]{:S(2)}) async-start(), calls=%async_computation.14 | async-start | bytes 2621440 | tf_op jit(solution)/shard_map/reduce_scatter | solution.py:43
  220.1 34.0 %copy-start.12 = (f32[256]{0:T(256)S(1)}, f32[256]{0:T(256)}, u32[]{:S(2)}) copy-start(f32[256]{0:T(256)} %param.28) | copy-start | bytes 3076
  220.1 47.0 %copy-start.5 = (bf16[512,256]{1,0:T(8,128)(2,1)S(1)}, bf16[512,256]{1,0:T(8,128)(2,1)}, u32[]{:S(2)}) copy-start(bf16[512,256]{1,0:T(8,128)(2,1)} %param.31) | copy-start | bytes 786436
  220.1 47.0 %copy-start.10 = (f32[256]{0:T(256)S(1)}, f32[256]{0:T(256)}, u32[]{:S(2)}) copy-start(f32[256]{0:T(256)} %param.29) | copy-start | bytes 3076
  224.6 49.3 %copy-start.13 = (f32[256]{0:T(256)S(1)}, f32[256]{0:T(256)}, u32[]{:S(2)}) copy-start(f32[256]{0:T(256)} %param.30) | copy-start | bytes 3076
  224.7 69.7 %all-gather.18.cloned.1.call-start = ((), (), s32[]{:S(2)}) async-start(), calls=%async_computation.15 | async-start | bytes 1310720 | tf_op jit(solution)/shard_map/all_gather | solution.py:39
  276.6 57.2 %reduce-scatter.13.cloned.1.call-start = ((), (), s32[]{:S(2)}) async-start(), calls=%async_computation.16 | async-start | bytes 2621440 | tf_op jit(solution)/shard_map/reduce_scatter | solution.py:47
  294.3 5.6 copy-start.14
  298.9 1.0 copy-start.18
  302.5 57.2 %all-gather.20.cloned.1.call-start = ((), (), s32[]{:S(2)}) async-start(), calls=%async_computation.17 | async-start | bytes 1310720 | tf_op jit(solution)/shard_map/all_gather | solution.py:39
  342.2 4.4 copy-start.16
  342.2 63.6 %reduce-scatter.23.cloned.1.call-start = ((), (), s32[]{:S(2)}) async-start(), calls=%async_computation.22 | async-start | bytes 2621440 | tf_op jit(solution)/shard_map/reduce_scatter | solution.py:183
  346.5 104.2 %reduce-scatter.21.cloned.1.call-start = ((), (), s32[]{:S(2)}) async-start(), calls=%async_computation.21 | async-start | bytes 2621440 | tf_op jit(solution)/shard_map/reduce_scatter | solution.py:180
  350.4 124.2 %reduce-scatter.19.cloned.1.call-start = ((), (), s32[]{:S(2)}) async-start(), calls=%async_computation.20 | async-start | bytes 655360 | tf_op jit(solution)/shard_map/reduce_scatter | solution.py:177
  359.8 7.7 %copy-start.1 = (bf16[512,1024]{1,0:T(8,128)(2,1)S(1)}, bf16[512,1024]{1,0:T(8,128)(2,1)}, u32[]{:S(2)}) copy-start(bf16[512,1024]{1,0:T(8,128)(2,1)} %all-gather.20.cloned.1.call-done) | copy-start | bytes 3145732
  361.6 0.7 copy-start.7
  366.4 7.5 %copy-start.3 = (bf16[512,1,256]{0,2,1:T(8,128)(2,1)S(1)}, bf16[512,1,256]{0,2,1:T(8,128)(2,1)}, u32[]{:S(2)}) copy-start(bf16[512,1,256]{0,2,1:T(8,128)(2,1)} %copy-done.2) | copy-start | bytes 786436
  369.8 140.8 %reduce-scatter.17.cloned.1.call-start = ((), (), s32[]{:S(2)}) async-start(), calls=%async_computation.19 | async-start | bytes 1966080 | tf_op jit(solution)/shard_map/reduce_scatter | solution.py:174
  382.9 7.7 %copy-start.15 = (bf16[512,1024]{1,0:T(8,128)(2,1)S(1)}, bf16[512,1024]{1,0:T(8,128)(2,1)}, u32[]{:S(2)}) copy-start(bf16[512,1024]{1,0:T(8,128)(2,1)} %all-gather.8.cloned.1.call-done) | copy-start | bytes 3145732
  392.8 153.2 %reduce-scatter.15.cloned.1.call-start = ((), (), s32[]{:S(2)}) async-start(), calls=%async_computation.18 | async-start | bytes 2621440 | tf_op jit(solution)/shard_map/reduce_scatter | solution.py:47
  396.6 200.3 %all-reduce.6.cloned.1.call-start = ((), (), s32[]{:S(2)}) async-start(), calls=%async_computation.23 | async-start | bytes 3145728 | tf_op jit(solution)/shard_map/psum | solution.py:188
Sparse Core Ops, SparseCore 0:
  9.5 19.5 all-gather.7
  31.2 37.6 all-gather.9
  78.3 29.3 reduce-scatter.8
  109.1 45.6 all-gather.13
  156.8 15.6 all-gather.11
  173.8 46.2 all-gather.15
  224.8 29.3 reduce-scatter.10
  276.8 17.5 all-gather.17
  302.6 31.1 reduce-scatter.12
  342.3 17.4 all-gather.19
  362.1 43.6 reduce-scatter.22
  407.9 42.8 reduce-scatter.20
  453.6 21.0 reduce-scatter.18
  476.8 33.6 reduce-scatter.16
  512.9 29.9 reduce-scatter.14
  545.3 51.5 all-reduce.5
where the time goes:
time: 612 us; the launch traced here: 611 us
  waiting for transfers between devices  413 us (67%)
  blocking collectives  87.8 us (14%)
  matrix products  65.8 us (11%)
  other arithmetic  19.2 us (3%)
  between operations  14.2 us (2%)
  local copies, waits for them, and re-layouts  10.1 us (2%)
    reduce_scatter x2, waiting for transfers between devices, collect(): return lax.psum_scatter(partial_sum, 'col', scatter_dimension=1, tiled=True)  58.4 us
    psum x1, waiting for transfers between devices, per_device(): lax.psum(pieces[0].astype(jnp.bfloat16), 'dp').astype(jnp.float32)  49 us
    reduce_scatter x1, waiting for transfers between devices, per_device(): lax.psum_scatter(wup_part.astype(jnp.bfloat16), 'row', scatter_dimension=...  45 us
    all_gather x1, waiting for transfers between devices, per_device(): lax.all_gather(w_down, 'row', axis=1, tiled=True)  42.8 us
    all_gather x1, waiting for transfers between devices, per_device(): lax.all_gather(w_qkv, 'row', axis=0, tiled=True)  38.9 us
    reduce_scatter x1, waiting for transfers between devices, per_device(): lax.psum_scatter(wqkv_part.astype(jnp.bfloat16), 'row', scatter_dimension...  35.9 us
    psum x1, blocking collectives, per_device(): lax.psum((qbias_part, vbias_part, obias_part, ngain_part, nshift_part, ub...  35.2 us
    all_gather x1, waiting for transfers between devices, per_device(): lax.all_gather(w_up, 'row', axis=0, tiled=True)  32.7 us
  transfers between devices with their start and end apart: 16, of which 14 were waited for; matrix products, arithmetic and copies ran while one was open for 9% of the time, Pallas kernels for 0%

commit v1 on v0

--- a/solution.py
+++ b/solution.py
@@ -8,6 +8,27 @@
 EPS = 1e-12
 INV_ROOT_TWO = 0.7071067811865476
 INV_ROOT_PI = 0.3989422804014327
+
+
+def collect_2(x, axis, dim):
+    peers, index, rows = (lax.axis_size(axis), lax.axis_index(axis), x.shape[dim])
+    upward = [(i, (i + 1) % peers) for i in range(peers)]
+    backward = [(i, (i - 1) % peers) for i in range(peers)]
+    result = jnp.zeros((*x.shape[:dim], peers * rows, *x.shape[dim + 1 :]), x.dtype)
+    result = lax.dynamic_update_slice_in_dim(result, x, index * rows, axis=dim)
+    from_left = from_right = x
+    half = peers // 2
+    for step in range(1, half + 1):
+        from_left = lax.ppermute(from_left, axis, upward)
+        result = lax.dynamic_update_slice_in_dim(
+            result, from_left, (index - step) % peers * rows, axis=dim
+        )
+        if step < peers - half:
+            from_right = lax.ppermute(from_right, axis, backward)
+            result = lax.dynamic_update_slice_in_dim(
+                result, from_right, (index + step) % peers * rows, axis=dim
+            )
+    return result
 
 
 def gelu_parts(pre_act):
@@ -104,7 +125,7 @@
     qkv_full, out_full, up_full, down_full = (
         lax.all_gather(w_qkv, "row", axis=0, tiled=True),
         lax.all_gather(w_out, "row", axis=1, tiled=True),
-        lax.all_gather(w_up, "row", axis=0, tiled=True),
+        collect_2(w_up, "row", 0),
         lax.all_gather(w_down, "row", axis=1, tiled=True),
     )
     tokens_dev = hidden_in.shape[0]

time: 612 us -> 587 us (0.959)
  waiting for transfers between devices: 413 us -> 377 us
  local copies, waits for them, and re-layouts: 10.1 us -> 18.1 us
    ppermute x0 -> x3, waiting for transfers between devices: none -> 36.3 us  [the longest x2 30.4 us: collect_2(): from_left = lax.ppermute(from_left, axis, upward)]
    all_gather x1 -> x0, waiting for transfers between devices: 32.7 us -> none  [per_device(): lax.all_gather(w_up, 'row', axis=0, tiled=True)]
    all_gather x1, waiting for transfers between devices: 42.8 us -> 19.1 us  [per_device(): lax.all_gather(w_down, 'row', axis=1, tiled=True)]
    all_gather x2, waiting for transfers between devices: 17.7 us -> 0.02 us  [spread(): return lax.all_gather(block, 'col', axis=1, tiled=True)]
    dynamic_update_slice x0 -> x4, local copies, waits for them, and re-layouts: none -> 6.57 us  [the longest x2 3.73 us: collect_2(): lax.dynamic_update_slice_in_dim(result, from_left, (index - step) % peers...]
  transfers between devices with their start and end apart: 16 -> 18, of which waited for: 14 -> 15; matrix products, arithmetic and copies ran while one was open for 9% -> 11% of each run, Pallas kernels for 0% -> 0%
where the time goes in v1:
time: 587 us; the launch traced here: 586 us
  waiting for transfers between devices  377 us (64%)
  blocking collectives  87.7 us (15%)
  matrix products  66 us (11%)
  local copies, waits for them, and re-layouts  18.1 us (3%)
  other arithmetic  17.4 us (3%)
  between operations  14.2 us (2%)
    reduce_scatter x2, waiting for transfers between devices, collect(): return lax.psum_scatter(partial_sum, 'col', scatter_dimension=1, tiled=True)  59.5 us
    psum x1, waiting for transfers between devices, per_device(): lax.psum(pieces[0].astype(jnp.bfloat16), 'dp').astype(jnp.float32)  49 us
    reduce_scatter x1, waiting for transfers between devices, per_device(): lax.psum_scatter(wup_part.astype(jnp.bfloat16), 'row', scatter_dimension=...  45.2 us
    all_gather x1, waiting for transfers between devices, per_device(): lax.all_gather(w_qkv, 'row', axis=0, tiled=True)  39.7 us
    reduce_scatter x1, waiting for transfers between devices, per_device(): lax.psum_scatter(wqkv_part.astype(jnp.bfloat16), 'row', scatter_dimension...  36 us
    psum x1, blocking collectives, per_device(): lax.psum((qbias_part, vbias_part, obias_part, ngain_part, nshift_part, ub...  35.2 us
    reduce_scatter x2, waiting for transfers between devices, collect_back(): return lax.psum_scatter(partial_sum, 'col', scatter_dimension=1, tiled=True)  31.3 us
    ppermute x2, waiting for transfers between devices, collect_2(): from_left = lax.ppermute(from_left, axis, upward)  30.4 us
  transfers between devices with their start and end apart: 18, of which 15 were waited for; matrix products, arithmetic and copies ran while one was open for 11% of the time, Pallas kernels for 0%

profile of v1, /device:TPU:0, one launch (start us, length us, event | category | flops | bytes accessed | tf_op | source)
XLA Modules:
  0.0 585.8 jit_solution(3017682937167523054)
XLA Ops:
  8.0 1.9 copy.31
  10.0 0.8 add.190
  11.5 17.6 %all_gather.23 = bf16[256,1024]{1,0:T(8,128)(2,1)S(1)} all-gather(bf16[256,256]{1,0:T(8,128)(2,1)} %param.21), channel_id=1, replica_groups=mesh['dp'=2,'row'=4,'col'=4] {'row'}, dimensions={1}, use_global_device_ids=true | all-gather | bytes 655360 | tf_op jit(solution)/shard_map/all_gather | solution.py:127
  29.3 39.7 %all-gather.9.cloned.1.call-done = bf16[1024,3,256]{0,2,1:T(8,128)(2,1)} async-done(((bf16[256,3,256]{0,2,1:T(8,128)(2,1)}), bf16[1024,3,256]{0,2,1:T(8,128)(2,1)}) %all-gather.9.cloned.1.call-update) | async-done | bytes 1572880 | tf_op jit(solution)/shard_map/all_gather | solution.py:126
  69.0 2.7 fusion.26
  71.8 0.9 fusion.2
  72.8 0.9 exponential_reduce_fusion
  73.7 1.0 copy-done
  74.7 1.3 convolution_convert_fusion.5
  76.0 1.8 fusion.61
  77.9 29.5 %reduce-scatter.9.cloned.1.call-done = f32[512,256]{1,0:T(8,128)} async-done(((f32[512,1024]{1,0:T(8,128)}), f32[512,256]{1,0:T(8,128)}) %reduce-scatter.9.cloned.1.call-update) | async-done | bytes 524304 | tf_op jit(solution)/shard_map/reduce_scatter | solution.py:64
  107.4 1.2 fusion.55
  108.6 5.8 psum.147
  114.6 5.7 psum.148
  120.3 0.9 fusion.40
  121.9 1.7 collective-permute-start
  123.6 2.2 collective-permute-start.1
  125.7 12.9 %collective-permute-done = bf16[256,1024]{1,0:T(8,128)(2,1)} collective-permute-done((bf16[256,1024]{1,0:T(8,128)(2,1)S(1)}, bf16[256,1024]{1,0:T(8,128)(2,1)}, u32[]{:S(2)}, u32[]{:S(2)}) %collective-permute-start) | collective-permute-done | bytes 524320 | tf_op jit(solution)/shard_map/ppermute | solution.py:22
  138.7 1.7 broadcast_in_dim.79
  140.3 0.9 constant_dynamic-update-slice_fusion.3
  141.2 1.9 constant_dynamic-update-slice_fusion.2
  143.1 5.9 %collective-permute-done.1 = bf16[256,1024]{1,0:T(8,128)(2,1)} collective-permute-done((bf16[256,1024]{1,0:T(8,128)(2,1)S(1)}, bf16[256,1024]{1,0:T(8,128)(2,1)}, u32[]{:S(2)}, u32[]{:S(2)}) %collective-permute-start.1) | collective-permute-done | bytes 524320 | tf_op jit(solution)/shard_map/ppermute | solution.py:27
  148.9 2.0 constant_dynamic-update-slice_fusion.1
  150.9 17.5 %collective-permute-done.2 = bf16[256,1024]{1,0:T(8,128)(2,1)} collective-permute-done((bf16[256,1024]{1,0:T(8,128)(2,1)}, bf16[256,1024]{1,0:T(8,128)(2,1)}, u32[]{:S(2)}, u32[]{:S(2)}) %collective-permute-start.2) | collective-permute-done | bytes 524320 | tf_op jit(solution)/shard_map/ppermute | solution.py:22
  168.4 1.9 constant_dynamic-update-slice_fusion
  170.3 4.6 multiply_convert_fusion.1
  174.9 19.1 %all-gather.13.cloned.1.call-done = bf16[1024,1024]{1,0:T(8,128)(2,1)} async-done(((bf16[1024,256]{1,0:T(8,128)(2,1)}), bf16[1024,1024]{1,0:T(8,128)(2,1)}) %all-gather.13.cloned.1.call-update) | async-done | bytes 2097168 | tf_op jit(solution)/shard_map/all_gather | solution.py:129
  194.0 4.1 fusion.62
  198.2 30.0 %reduce-scatter.11.cloned.1.call-done = f32[512,256]{1,0:T(8,128)} async-done(((f32[512,1024]{1,0:T(8,128)}), f32[512,256]{1,0:T(8,128)}) %reduce-scatter.11.cloned.1.call-update) | async-done | bytes 524304 | tf_op jit(solution)/shard_map/reduce_scatter | solution.py:64
  228.2 1.3 fusion.54
  229.6 5.8 psum.149
  235.6 5.7 psum.150
  241.6 6.3 %all-reduce.2 = (f32[512]{0:T(512)S(1)}, f32[512]{0:T(512)S(1)}) all-reduce(f32[512]{0:T(512)S(1)} %get-tuple-element.84, f32[512]{0:T(512)S(1)} %get-tuple-element.87), channel_id=1, replica_groups=mesh['dp'=2,'row'=4,'col'=4] {'col'}, use_global_device_ids=true, to_apply=%region_15.16 | all-reduce | flops 1024 | bytes 8192 | tf_op jit(solution)/shard_map/psum | solution.py:51
  248.0 2.0 fusion.49
  250.9 17.5 %all-gather.15.cloned.1.call-done = bf16[512,1024]{1,0:T(8,128)(2,1)} async-done(((bf16[512,256]{1,0:T(8,128)(2,1)}), bf16[512,1024]{1,0:T(8,128)(2,1)}) %all-gather.15.cloned.1.call-update) | async-done | bytes 1048592 | tf_op jit(solution)/shard_map/all_gather | solution.py:60
  268.4 4.4 fusion.51
  272.8 1.0 copy-done.20
  273.8 4.3 fusion.38
  278.1 31.3 %reduce-scatter.13.cloned.1.call-done = f32[512,256]{1,0:T(8,128)} async-done(((f32[512,1024]{1,0:T(8,128)}), f32[512,256]{1,0:T(8,128)}) %reduce-scatter.13.cloned.1.call-update) | async-done | bytes 524304 | tf_op jit(solution)/shard_map/reduce_scatter | solution.py:68
  309.4 1.4 multiply_reduce_fusion.1
  310.8 5.8 all-reduce.1
  317.8 4.2 convolution_convert_fusion
  322.1 4.1 convolution_convert_fusion.1
  326.3 9.0 %all-gather.17.cloned.1.call-done = bf16[512,1024]{1,0:T(8,128)(2,1)} async-done(((bf16[512,256]{1,0:T(8,128)(2,1)}), bf16[512,1024]{1,0:T(8,128)(2,1)}) %all-gather.17.cloned.1.call-update) | async-done | bytes 1048592 | tf_op jit(solution)/shard_map/all_gather | solution.py:60
  335.3 1.7 convolution_convert_fusion.4
  337.0 4.2 fusion.57
  341.2 1.8 copy.38
  343.0 1.2 convolution_convert_fusion.3
  344.6 2.9 fusion.41
  347.5 8.8 %fusion.58 = (f32[4,64]{1,0:T(4,128)S(1)}, bf16[512,4,64]{0,2,1:T(8,128)(2,1)S(1)}) fusion(bf16[512,4,64]{0,2,1:T(8,128)(2,1)S(1)} %bitcast.55, f32[4,512,512]{1,2,0:T(8,128)} %fusion.41, f32[4,512]{1,0:T(4,128)S(1)} %log_add_fusion, f32[4,512,512]{1,2,0:T(8,128)} %copy-done, pred[512,512]{0,1:T(8,128)(4,1)S(1)} %broadcast_compare_fusion), kind=kOutput, calls=%fused_computation.95 | convolution fusion | flops 146016512 | bytes 9184256 | tf_op jit(solution)/shard_map/while/body/eval_jaxpr/hqk,khd->qhd/dot_general | solution.py:100
  356.4 7.5 %fusion.22 = bf16[4,64,512]{2,1,0:T(8,128)(2,1)S(1)} fusion(f32[4,512,512]{1,2,0:T(8,128)} %fusion.41, f32[512,4,64]{0,2,1:T(8,128)S(1)} %bitcast.51, f32[4,64]{1,0:T(4,128)S(1)} %add.190, f32[4,512,512]{1,2,0:T(8,128)} %copy-done, f32[4,512]{1,0:T(4,128)S(1)} %log_add_fusion, pred[512,512]{0,1:T(8,128)(4,1)S(1)} %broadcast_compare_fusion), kind=kOutput, calls=%fused_computation.28 | convolution fusion | flops 146147840 | bytes 9446400 | tf_op jit(solution)/shard_map/while/body/eval_jaxpr/hqk,qhd->khd/dot_general | solution.py:101
  364.1 3.4 fusion.18
  367.6 3.7 convolution_bitcast_fusion
  371.4 9.7 %reduce-scatter.23.cloned.1.call-done = bf16[1024,256]{1,0:T(8,128)(2,1)} async-done(((bf16[1024,1024]{1,0:T(8,128)(2,1)}), bf16[1024,256]{1,0:T(8,128)(2,1)}) %reduce-scatter.23.cloned.1.call-update) | async-done | bytes 524304 | tf_op jit(solution)/shard_map/reduce_scatter | solution.py:204
  381.1 45.2 %reduce-scatter.21.cloned.1.call-done = bf16[256,1024]{1,0:T(8,128)(2,1)} async-done(((bf16[1024,1024]{1,0:T(8,128)(2,1)}), bf16[256,1024]{1,0:T(8,128)(2,1)}) %reduce-scatter.21.cloned.1.call-update) | async-done | bytes 524304 | tf_op jit(solution)/shard_map/reduce_scatter | solution.py:201
  426.3 23.8 %reduce-scatter.19.cloned.1.call-done = bf16[256,256]{1,0:T(8,128)(2,1)} async-done(((bf16[256,1024]{1,0:T(8,128)(2,1)}), bf16[256,256]{1,0:T(8,128)(2,1)}) %reduce-scatter.19.cloned.1.call-update) | async-done | bytes 131088 | tf_op jit(solution)/shard_map/reduce_scatter | solution.py:198
  450.0 36.0 %reduce-scatter.17.cloned.1.call-done = bf16[256,3,256]{0,2,1:T(8,128)(2,1)} async-done(((bf16[1024,3,256]{0,2,1:T(8,128)(2,1)}), bf16[256,3,256]{0,2,1:T(8,128)(2,1)}) %reduce-scatter.17.cloned.1.call-update) | async-done | bytes 393232 | tf_op jit(solution)/shard_map/reduce_scatter | solution.py:195
  486.3 35.2 %all-reduce = (f32[256]{0:T(256)}, f32[256]{0:T(256)}, f32[256]{0:T(256)}, f32[256]{0:T(256)}, f32[256]{0:T(256)}, /*index=5*/f32[1024]{0:T(1024)}, f32[256]{0:T(256)}, f32[256]{0:T(256)}, f32[256]{0:T(256)}) all-reduce(f32[256]{0:T(256)S(1)} %reduce_sum.188, ...), channel_id=1, replica_groups=mesh['dp'=2,'row'=4,'col'=4] {'dp','row'}, use_global_device_ids=true, to_apply=%region_26.27 | all-reduce | flops 3072 | bytes 24576 | tf_op jit(solution)/shard_map/psum | solution.py:214
  521.5 1.9 add.220
  523.4 49.0 %all-reduce.6.cloned.1.call-done = (bf16[256,3,256]{0,2,1:T(8,128)(2,1)}, bf16[256,256]{1,0:T(8,128)(2,1)}, bf16[256,1024]{1,0:T(8,128)(2,1)}, bf16[1024,256]{1,0:T(8,128)(2,1)}) async-done(((bf16[256,3,256]{0,2,1:T(8,128)(2,1)}, bf16[256,256]{1,0:T(8,128)(2,1)}, bf16[256,1024]{1,0:T(8,128)(2,1)}, bf16[1024,256]{1,0:T(8,128)(2,1)}), (bf16[256,3,256]{0,2,1:T(8,128)(2,1)}, bf16[256,256]{1,0:T(8,128)(2,1)}, ...) | async-done | bytes 1572880 | tf_op jit(solution)/shard_map/psum | solution.py:209
  572.4 1.7 convert_element_type.113
  574.1 2.0 copy.41
  576.1 2.1 convert_element_type.115
  578.3 1.0 convert_element_type.117
  (96 shorter events, 6.8 us)
Async XLA Ops:
  7.2 21.9 %copy-start.12 = (s32[1,512]{1,0:T(1,128)S(1)}, s32[1,512]{1,0:T(1,128)}, u32[]{:S(2)}) copy-start(s32[1,512]{1,0:T(1,128)} %param.17) | copy-start | bytes 6148
  7.2 22.1 %all-gather.7.cloned.1.call-start = ((), (), s32[]{:S(2)}) async-start(), calls=%async_computation.8 | async-start | bytes 1310720 | tf_op jit(solution)/shard_map/all_gather | solution.py:56
  7.9 61.1 %all-gather.9.cloned.1.call-start = ((), (), s32[]{:S(2)}) async-start(), calls=%async_computation.9 | async-start | bytes 1966080 | tf_op jit(solution)/shard_map/all_gather | solution.py:126
  9.9 97.5 %reduce-scatter.9.cloned.1.call-start = ((), (), s32[]{:S(2)}) async-start(), calls=%async_computation.10 | async-start | bytes 2621440 | tf_op jit(solution)/shard_map/reduce_scatter | solution.py:64
  71.8 1.0 copy-start.2
  72.8 1.9 copy-start
  76.0 1.9 copy-start.6
  76.0 31.4 %copy-start.4 = (bf16[512,256]{1,0:T(8,128)(2,1)S(1)}, bf16[512,256]{1,0:T(8,128)(2,1)}, u32[]{:S(2)}) copy-start(bf16[512,256]{1,0:T(8,128)(2,1)} %param.16) | copy-start | bytes 786436
  76.0 31.4 %copy-start.15 = (f32[256]{0:T(256)S(1)}, f32[256]{0:T(256)}, u32[]{:S(2)}) copy-start(f32[256]{0:T(256)} %param.22) | copy-start | bytes 3076
  77.8 42.4 %copy-start.11 = (f32[256]{0:T(256)S(1)}, f32[256]{0:T(256)}, u32[]{:S(2)}) copy-start(f32[256]{0:T(256)} %param.23) | copy-start | bytes 3076
  77.8 42.4 %copy-start.13 = (f32[256]{0:T(256)S(1)}, f32[256]{0:T(256)}, u32[]{:S(2)}) copy-start(f32[256]{0:T(256)} %param.24) | copy-start | bytes 3076
  77.9 44.0 %copy-start.9 = (bf16[256,1024]{1,0:T(8,128)(2,1)S(1)}, bf16[256,1024]{1,0:T(8,128)(2,1)}, u32[]{:S(2)}) copy-start(bf16[256,1024]{1,0:T(8,128)(2,1)} %param.25) | copy-start | bytes 1572868
  77.9 92.4 %all-gather.11.cloned.1.call-start = ((), (), s32[]{:S(2)}) async-start(), calls=%async_computation.11 | async-start | bytes 1310720 | tf_op jit(solution)/shard_map/all_gather | solution.py:56
  121.2 72.8 %all-gather.13.cloned.1.call-start = ((), (), s32[]{:S(2)}) async-start(), calls=%async_computation.12 | async-start | bytes 2621440 | tf_op jit(solution)/shard_map/all_gather | solution.py:129
  121.8 106.4 %reduce-scatter.11.cloned.1.call-start = ((), (), s32[]{:S(2)}) async-start(), calls=%async_computation.13 | async-start | bytes 2621440 | tf_op jit(solution)/shard_map/reduce_scatter | solution.py:64
  121.9 16.8 %collective-permute-start = (bf16[256,1024]{1,0:T(8,128)(2,1)S(1)}, bf16[256,1024]{1,0:T(8,128)(2,1)}, u32[]{:S(2)}, u32[]{:S(2)}) collective-permute-start(bf16[256,1024]{1,0:T(8,128)(2,1)S(1)} %copy-done.9), channel_id=1, source_target_pairs={{0,4},{4,8},{8,12},{12,0},{1,5},{5,9},{9,13},{13,1},{2,6},{6,10},{... | collective-permute-start | bytes 1572872 | tf_op jit(solution)/shard_map/ppermute | solution.py:22
  123.6 25.4 %collective-permute-start.1 = (bf16[256,1024]{1,0:T(8,128)(2,1)S(1)}, bf16[256,1024]{1,0:T(8,128)(2,1)}, u32[]{:S(2)}, u32[]{:S(2)}) collective-permute-start(bf16[256,1024]{1,0:T(8,128)(2,1)S(1)} %copy-done.9), channel_id=1, source_target_pairs={{0,12},{4,0},{8,4},{12,8},{1,13},{5,1},{9,5},{13,9},{2,14},{6,2},{... | collective-permute-start | bytes 1572872 | tf_op jit(solution)/shard_map/ppermute | solution.py:27
  138.7 29.7 %collective-permute-start.2 = (bf16[256,1024]{1,0:T(8,128)(2,1)}, bf16[256,1024]{1,0:T(8,128)(2,1)}, u32[]{:S(2)}, u32[]{:S(2)}) collective-permute-start(bf16[256,1024]{1,0:T(8,128)(2,1)} %collective-permute-done), channel_id=1, source_target_pairs={{0,4},{4,8},{8,12},{12,0},{1,5},{5,9},{9,13},{13,1},{2,6},{6,10},{... | collective-permute-start | bytes 1572872 | tf_op jit(solution)/shard_map/ppermute | solution.py:22
  140.3 30.0 %copy-start.18 = (f32[1024]{0:T(1024)S(1)}, f32[1024]{0:T(1024)}, u32[]{:S(2)}) copy-start(f32[1024]{0:T(1024)} %param.26) | copy-start | bytes 12292
  174.9 23.2 %copy-start.19 = (bf16[512,1024]{1,0:T(8,128)(2,1)}, bf16[512,1024]{1,0:T(8,128)(2,1)S(1)}, u32[]{:S(2)}) copy-start(bf16[512,1024]{1,0:T(8,128)(2,1)S(1)} %get-tuple-element.126) | copy-start | bytes 3145732
  198.1 30.1 %copy-start.16 = (f32[256]{0:T(256)S(1)}, f32[256]{0:T(256)}, u32[]{:S(2)}) copy-start(f32[256]{0:T(256)} %param.28) | copy-start | bytes 3076
  198.1 43.1 %copy-start.5 = (bf16[512,256]{1,0:T(8,128)(2,1)S(1)}, bf16[512,256]{1,0:T(8,128)(2,1)}, u32[]{:S(2)}) copy-start(bf16[512,256]{1,0:T(8,128)(2,1)} %param.31) | copy-start | bytes 786436
  198.1 43.1 %copy-start.14 = (f32[256]{0:T(256)S(1)}, f32[256]{0:T(256)}, u32[]{:S(2)}) copy-start(f32[256]{0:T(256)} %param.29) | copy-start | bytes 3076
  198.1 49.8 %copy-start.17 = (f32[256]{0:T(256)S(1)}, f32[256]{0:T(256)}, u32[]{:S(2)}) copy-start(f32[256]{0:T(256)} %param.30) | copy-start | bytes 3076
  198.2 70.2 %all-gather.15.cloned.1.call-start = ((), (), s32[]{:S(2)}) async-start(), calls=%async_computation.14 | async-start | bytes 1310720 | tf_op jit(solution)/shard_map/all_gather | solution.py:60
  250.7 58.7 %reduce-scatter.13.cloned.1.call-start = ((), (), s32[]{:S(2)}) async-start(), calls=%async_computation.15 | async-start | bytes 2621440 | tf_op jit(solution)/shard_map/reduce_scatter | solution.py:68
  272.8 1.0 copy-start.20
  278.1 57.2 %all-gather.17.cloned.1.call-start = ((), (), s32[]{:S(2)}) async-start(), calls=%async_computation.16 | async-start | bytes 1310720 | tf_op jit(solution)/shard_map/all_gather | solution.py:60
  317.7 63.4 %reduce-scatter.23.cloned.1.call-start = ((), (), s32[]{:S(2)}) async-start(), calls=%async_computation.21 | async-start | bytes 2621440 | tf_op jit(solution)/shard_map/reduce_scatter | solution.py:204
  322.0 104.2 %reduce-scatter.21.cloned.1.call-start = ((), (), s32[]{:S(2)}) async-start(), calls=%async_computation.20 | async-start | bytes 2621440 | tf_op jit(solution)/shard_map/reduce_scatter | solution.py:201
  326.2 123.8 %reduce-scatter.19.cloned.1.call-start = ((), (), s32[]{:S(2)}) async-start(), calls=%async_computation.19 | async-start | bytes 655360 | tf_op jit(solution)/shard_map/reduce_scatter | solution.py:198
  337.0 6.0 %copy-start.1 = (bf16[512,1024]{1,0:T(8,128)(2,1)S(1)}, bf16[512,1024]{1,0:T(8,128)(2,1)}, u32[]{:S(2)}) copy-start(bf16[512,1024]{1,0:T(8,128)(2,1)} %all-gather.17.cloned.1.call-done) | copy-start | bytes 3145732
  337.0 6.0 %copy-start.7 = (bf16[4,64,512]{2,1,0:T(8,128)(2,1)S(1)}, bf16[4,64,512]{2,1,0:T(8,128)(2,1)}, u32[]{:S(2)}) copy-start(bf16[4,64,512]{2,1,0:T(8,128)(2,1)} %copy-done.6) | copy-start | bytes 786436
  344.3 3.2 copy-start.3
  344.3 141.8 %reduce-scatter.17.cloned.1.call-start = ((), (), s32[]{:S(2)}) async-start(), calls=%async_computation.18 | async-start | bytes 1966080 | tf_op jit(solution)/shard_map/reduce_scatter | solution.py:195
  356.4 7.7 %copy-start.10 = (bf16[512,1,256]{2,0,1:T(8,128)(2,1)S(1)}, bf16[512,1,256]{2,0,1:T(8,128)(2,1)}, u32[]{:S(2)}) copy-start(bf16[512,1,256]{2,0,1:T(8,128)(2,1)} %copy.38) | copy-start | bytes 786436
  367.5 154.0 %reduce-scatter.15.cloned.1.call-start = ((), (), s32[]{:S(2)}) async-start(), calls=%async_computation.17 | async-start | bytes 2621440 | tf_op jit(solution)/shard_map/reduce_scatter | solution.py:68
  371.3 201.1 %all-reduce.6.cloned.1.call-start = ((), (), s32[]{:S(2)}) async-start(), calls=%async_computation.22 | async-start | bytes 3145728 | tf_op jit(solution)/shard_map/psum | solution.py:209
  572.4 5.9 %copy-start.8 = (bf16[1024,256]{1,0:T(8,128)(2,1)S(1)}, bf16[1024,256]{1,0:T(8,128)(2,1)}, u32[]{:S(2)}) copy-start(bf16[1024,256]{1,0:T(8,128)(2,1)} %get-tuple-element.105) | copy-start | bytes 1572868
Sparse Core Ops, SparseCore 0:
  9.5 19.5 all-gather.6
  31.3 37.6 all-gather.8
  78.0 29.3 reduce-scatter.8
  121.3 17.6 all-gather.10
  140.4 53.5 all-gather.12
  198.3 29.8 reduce-scatter.10
  250.8 17.5 all-gather.14
  278.2 31.1 reduce-scatter.12
  317.8 17.4 all-gather.16
  337.4 43.6 reduce-scatter.22
  383.4 42.8 reduce-scatter.20
  429.0 21.0 reduce-scatter.18
  452.3 33.6 reduce-scatter.16
  488.5 29.9 reduce-scatter.14
  520.8 51.5 all-reduce.5
